TPU v7x, 32 devices: a whole 2x2x4 slice. The times are simulated.
32 devices in a mesh: row: 4 (over x, core), col: 8 (over z, y).
Axes of the slice: x: 2, y: 2, z: 4, core: 2. Of those that a mesh axis runs over, the one named last changes fastest.
Arguments:
- vectors: bfloat16 [32, 8192], P(None, ('row', 'col')), may hold values from -6 to 6
- tiles: bfloat16 [512, 256, 256], P(('row', 'col')), may hold values from -0.09375 to 0.09375
- tile_rows: int32 [512], P(('row', 'col')), may hold values from 0 to 7, as said below
- tile_cols: int32 [512], P(('row', 'col')), may hold values from 0 to 3, as said below
- tile_live: int32 [32], P(('row', 'col')), may hold values from 2 to 16, as said below
Outputs:
- first: bfloat16 [32, 8192], P(None, ('row', 'col'))
- second: bfloat16 [32, 8192], P(None, ('row', 'col'))
Inputs may be any that keep to these rules, and one draw needn't show every extreme that they name: `tile_rows`: A slot's row block is counted among the 8 row blocks of its device's row index, and its global row block never exceeds its global column block. `tile_cols`: A slot's column block is counted among the 4 column blocks of its device's column index. Each device uses its first tile_live slots; some device uses all 16.
All inputs are finite; a program needn't handle non-finite values.
Results may differ from a plain program's by a relative error of at most 0.0044.
Values may be sent and summed in bfloat16 or wider, within the bound.
No kernel may reach another device: no remote copies, remote signals or barrier semaphores. Data moves between devices by JAX's collectives and lax.ppermute only.
A program may use at most 64 MiB of HBM per device.

v0:
```python
import jax
import jax.numpy as jnp
from jax import lax
from jax.sharding import PartitionSpec as P


def half_direct(colset, tiles, rows, keep, count_rows):
    width = colset.shape[0]
    size = tiles.shape[1]
    picked = jnp.take(colset.reshape(width, -1, size), rows[1], axis=1)
    direct = jnp.einsum("ktj,tij->kti", picked, tiles, preferred_element_type=jnp.float32)
    row_hot = (rows[0][:, None] == jnp.arange(count_rows, dtype=jnp.int32)[None, :]).astype(
        jnp.float32
    ) * keep[:, None]
    placed = jnp.einsum("kti,ta->kai", direct, row_hot, precision=lax.Precision.HIGHEST)
    return placed.reshape(width, count_rows * size)


def half_mirror(rowset, tiles, cols, keep, count_cols):
    width = rowset.shape[0]
    size = tiles.shape[1]
    picked = jnp.take(rowset.reshape(width, -1, size), cols[1], axis=1)
    mirror = jnp.einsum("kti,tij->ktj", picked, tiles, preferred_element_type=jnp.float32)
    col_hot = (cols[0][:, None] == jnp.arange(count_cols, dtype=jnp.int32)[None, :]).astype(
        jnp.float32
    ) * keep[:, None]
    placed = jnp.einsum("ktj,tb->kbj", mirror, col_hot, precision=lax.Precision.HIGHEST)
    return placed.reshape(width, count_cols * size)


def sum_rows(direct):
    return lax.psum_scatter(direct, "col", scatter_dimension=1, tiled=True)


def sum_cols(mirror):
    return lax.psum_scatter(mirror, "row", scatter_dimension=1, tiled=True)


def gather_rowset(vec):
    return lax.all_gather(vec, "col", axis=1, tiled=True)


def both_halves(vec, rowset, tiles, tile_rows, tile_cols, tile_live):
    size = tiles.shape[1]
    count = tiles.shape[0]
    keep = (jnp.arange(count, dtype=jnp.int32) < tile_live[0]).astype(jnp.float32)
    colset = lax.all_gather(vec, "row", axis=1, tiled=True)
    count_rows = rowset.shape[1] // size
    count_cols = colset.shape[1] // size
    direct = half_direct(colset, tiles, (tile_rows, tile_cols), keep, count_rows)
    mirror = half_mirror(rowset, tiles, (tile_cols, tile_rows), keep, count_cols)
    return (direct, sum_cols(mirror))


def local(vectors, tiles, tile_rows, tile_cols, tile_live):
    direct, own_cols = both_halves(
        vectors, gather_rowset(vectors), tiles, tile_rows, tile_cols, tile_live
    )
    first = (sum_rows(direct) + own_cols).astype(jnp.bfloat16)
    next_rowset = gather_rowset(first)
    direct_two, cols_two = both_halves(first, next_rowset, tiles, tile_rows, tile_cols, tile_live)
    second_f = 2.0 * (sum_rows(direct_two) + cols_two) - vectors.astype(jnp.float32)
    return (first, second_f.astype(jnp.bfloat16))


def solution(mesh):
    placed = (
        P(None, ("row", "col")),
        P(("row", "col"), None, None),
        P(("row", "col")),
        P(("row", "col")),
        P(("row", "col")),
    )
    return jax.shard_map(
        local,
        mesh=mesh,
        in_specs=placed,
        out_specs=(P(None, ("row", "col")), P(None, ("row", "col"))),
        check_vma=False,
    )
```

profile of v0, /device:TPU:0, one launch (start us, length us, event | category | flops | bytes accessed | tf_op | source)
XLA Modules:
  0.0 261.5 jit_solution(1111360292076652762)
XLA Ops:
  7.2 0.0 copy-start
  7.2 0.0 copy-start.3
  7.2 0.0 reduce-scatter.7.cloned.1.call-start
  7.2 0.8 compare_select_fusion
  8.0 0.7 compare_and_fusion
  9.4 32.5 %all_gather.13 = bf16[32,2048]{1,0:T(8,128)(2,1)S(1)} all-gather(bf16[32,256]{1,0:T(8,128)(2,1)} %param.9), channel_id=1, replica_groups=mesh['row'=4,'col'=8] {'col'}, dimensions={1}, use_global_device_ids=true | all-gather | bytes 147456 | tf_op jit(solution)/shard_map/all_gather | solution.py:40
  41.9 0.6 gather_fusion.1
  42.5 0.0 copy-done
  42.5 0.0 copy-start.2
  42.5 0.5 convolution_bitcast_fusion.2
  43.0 0.0 copy-done.3
  43.0 0.6 fusion.4
  43.7 0.0 copy-start.4
  43.7 0.7 copy.20
  44.3 0.0 reduce-scatter.7.cloned.1.call-update
  44.4 0.0 reduce-scatter.5.cloned.1.call-start
  44.4 0.0 copy-done.2
  44.4 5.2 %all_gather.12 = bf16[32,1024]{1,0:T(8,128)(2,1)S(1)} all-gather(bf16[32,256]{1,0:T(8,128)(2,1)S(1)} %copy-done.2), channel_id=1, replica_groups=mesh['row'=4,'col'=8] {'row'}, dimensions={1}, use_global_device_ids=true | all-gather | bytes 81920 | tf_op jit(solution)/shard_map/all_gather | solution.py:47
  49.7 0.6 gather_fusion
  50.3 0.7 convolution_bitcast_fusion.3
  51.0 0.0 copy-done.4
  51.0 0.7 fusion.6
  51.7 0.8 copy.19
  52.5 0.0 reduce-scatter.5.cloned.1.call-update
  52.5 0.0 reduce-scatter.11.cloned.1.call-start
  52.5 12.5 %reduce-scatter.7.cloned.1.call-done = f32[32,256]{1,0:T(8,128)} async-done(((f32[32,1024]{1,0:T(8,128)}), f32[32,256]{1,0:T(8,128)}) %reduce-scatter.7.cloned.1.call-update) | async-done | bytes 32784 | tf_op jit(solution)/shard_map/reduce_scatter | solution.py:36
  65.0 65.4 %reduce-scatter.5.cloned.1.call-done = f32[32,256]{1,0:T(8,128)} async-done(((f32[32,2048]{1,0:T(8,128)}), f32[32,256]{1,0:T(8,128)}) %reduce-scatter.5.cloned.1.call-update) | async-done | bytes 32784 | tf_op jit(solution)/shard_map/reduce_scatter | solution.py:32
  130.4 0.8 add_convert_fusion
  131.2 0.0 copy-start.1
  131.2 5.2 %all_gather.14 = bf16[32,1024]{1,0:T(8,128)(2,1)S(1)} all-gather(bf16[32,256]{1,0:T(8,128)(2,1)S(1)} %add_convert_fusion), channel_id=1, replica_groups=mesh['row'=4,'col'=8] {'row'}, dimensions={1}, use_global_device_ids=true | all-gather | bytes 81920 | tf_op jit(solution)/shard_map/all_gather | solution.py:47
  136.4 30.5 %all_gather.15 = bf16[32,2048]{1,0:T(8,128)(2,1)S(1)} all-gather(bf16[32,256]{1,0:T(8,128)(2,1)S(1)} %add_convert_fusion), channel_id=1, replica_groups=mesh['row'=4,'col'=8] {'col'}, dimensions={1}, use_global_device_ids=true | all-gather | bytes 147456 | tf_op jit(solution)/shard_map/all_gather | solution.py:40
  167.0 0.6 gather_fusion.2
  167.6 0.6 gather_fusion.3
  168.1 0.5 convolution_bitcast_fusion
  168.6 0.0 copy-done.1
  168.6 0.6 fusion
  169.3 0.7 copy.22
  170.0 0.0 reduce-scatter.11.cloned.1.call-update
  170.0 0.0 reduce-scatter.9.cloned.1.call-start
  170.0 0.7 convolution_bitcast_fusion.1
  170.7 0.7 fusion.2
  171.4 0.8 copy.21
  172.2 0.0 reduce-scatter.9.cloned.1.call-update
  172.2 16.5 %reduce-scatter.11.cloned.1.call-done = f32[32,256]{1,0:T(8,128)} async-done(((f32[32,1024]{1,0:T(8,128)}), f32[32,256]{1,0:T(8,128)}) %reduce-scatter.11.cloned.1.call-update) | async-done | bytes 32784 | tf_op jit(solution)/shard_map/reduce_scatter | solution.py:36
  188.7 64.9 %reduce-scatter.9.cloned.1.call-done = f32[32,256]{1,0:T(8,128)} async-done(((f32[32,2048]{1,0:T(8,128)}), f32[32,256]{1,0:T(8,128)}) %reduce-scatter.9.cloned.1.call-update) | async-done | bytes 32784 | tf_op jit(solution)/shard_map/reduce_scatter | solution.py:32
  253.6 1.4 subtract_convert_fusion
  (9 shorter events, 0.1 us)
Async XLA Ops:
  7.2 35.3 %copy-start = (bf16[16,256,256]{2,1,0:T(8,128)(2,1)S(1)}, bf16[16,256,256]{2,1,0:T(8,128)(2,1)}, u32[]{:S(2)}) copy-start(bf16[16,256,256]{2,1,0:T(8,128)(2,1)} %param.10) | copy-start | bytes 6291460
  7.2 35.8 %copy-start.3 = (s32[16]{0:T(128)S(1)}, s32[16]{0:T(128)}, u32[]{:S(2)}) copy-start(s32[16]{0:T(128)} %param.12) | copy-start | bytes 196
  7.2 57.8 %reduce-scatter.7.cloned.1.call-start = ((), (), s32[]{:S(2)}) async-start(), calls=%async_computation.5 | async-start | bytes 163840 | tf_op jit(solution)/shard_map/reduce_scatter | solution.py:36
  42.5 1.9 copy-start.2
  43.7 7.4 %copy-start.4 = (s32[16]{0:T(128)S(1)}, s32[16]{0:T(128)}, u32[]{:S(2)}) copy-start(s32[16]{0:T(128)} %param.11) | copy-start | bytes 196
  44.4 86.0 %reduce-scatter.5.cloned.1.call-start = ((), (), s32[]{:S(2)}) async-start(), calls=%async_computation.4 | async-start | bytes 294912 | tf_op jit(solution)/shard_map/reduce_scatter | solution.py:32
  52.5 136.2 %reduce-scatter.11.cloned.1.call-start = ((), (), s32[]{:S(2)}) async-start(), calls=%async_computation.7 | async-start | bytes 163840 | tf_op jit(solution)/shard_map/reduce_scatter | solution.py:36
  131.2 37.4 %copy-start.1 = (bf16[32,256]{1,0:T(8,128)(2,1)}, bf16[32,256]{1,0:T(8,128)(2,1)S(1)}, u32[]{:S(2)}) copy-start(bf16[32,256]{1,0:T(8,128)(2,1)S(1)} %add_convert_fusion) | copy-start | bytes 49156
  170.0 83.6 %reduce-scatter.9.cloned.1.call-start = ((), (), s32[]{:S(2)}) async-start(), calls=%async_computation.6 | async-start | bytes 294912 | tf_op jit(solution)/shard_map/reduce_scatter | solution.py:32
Sparse Core Ops, SparseCore 0:
  44.5 20.4 reduce-scatter.6
  68.7 61.6 reduce-scatter.4
  170.1 18.5 reduce-scatter.10
  191.9 61.6 reduce-scatter.8
where the time goes:
time: 262 us
  waiting for transfers between devices  159 us (61%)
  blocking collectives  73.5 us (28%)
  between operations  14.6 us (6%)
  local copies, waits for them, and re-layouts  5.23 us (2%)
  matrix products  5.03 us (2%)
  other arithmetic  3.65 us (1%)
    reduce_scatter x2, waiting for transfers between devices, sum_rows(): return lax.psum_scatter(direct, 'col', scatter_dimension=1, tiled=True)  130 us
    all_gather x2, blocking collectives, gather_rowset(): return lax.all_gather(vec, 'col', axis=1, tiled=True)  63 us
    reduce_scatter x2, waiting for transfers between devices, sum_cols(): return lax.psum_scatter(mirror, 'row', scatter_dimension=1, tiled=True)  29 us
    all_gather x2, blocking collectives, both_halves(): colset = lax.all_gather(vec, 'row', axis=1, tiled=True)  10.5 us
  transfers between devices with their start and end apart: 4, of which 4 were waited for; matrix products, arithmetic and copies ran while one was open for 2% of the time, Pallas kernels for 0%

commit v1 on v0

--- a/solution.py
+++ b/solution.py
@@ -2,6 +2,17 @@
 import jax.numpy as jnp
 from jax import lax
 from jax.sharding import PartitionSpec as P
+
+
+def press_the_panels(block_in):
+    parts_n = lax.axis_size("row")
+    oldest = [None] * parts_n
+    oldest[parts_n - 1] = block_in
+    lanes = tuple(((j0, (j0 + 1) % parts_n) for j0 in range(parts_n)))
+    for nth in range(parts_n - 2, -1, -1):
+        oldest[nth] = lax.ppermute(oldest[nth + 1], "row", lanes)
+    passed = jnp.concatenate(oldest, axis=1)
+    return jnp.roll(passed, shift=(lax.axis_index("row") + 1) * block_in.shape[1], axis=1)
 
 
 def half_direct(colset, tiles, rows, keep, count_rows):
@@ -44,7 +55,7 @@
     size = tiles.shape[1]
     count = tiles.shape[0]
     keep = (jnp.arange(count, dtype=jnp.int32) < tile_live[0]).astype(jnp.float32)
-    colset = lax.all_gather(vec, "row", axis=1, tiled=True)
+    colset = press_the_panels(vec)
     count_rows = rowset.shape[1] // size
     count_cols = colset.shape[1] // size
     direct = half_direct(colset, tiles, (tile_rows, tile_cols), keep, count_rows)

time: 262 us -> 259 us (0.989)
  blocking collectives: 73.5 us -> 62.9 us
  waiting for transfers between devices: 159 us -> 166 us
    ppermute x0 -> x6, waiting for transfers between devices: none -> 10.7 us  [press_the_panels(): oldest[nth] = lax.ppermute(oldest[nth + 1], 'row', lanes)]
    all_gather x2 -> x0, blocking collectives: 10.5 us -> none  [both_halves(): colset = lax.all_gather(vec, 'row', axis=1, tiled=True)]
    reduce_scatter x2, waiting for transfers between devices: 29 us -> 25.3 us  [sum_cols(): return lax.psum_scatter(mirror, 'row', scatter_dimension=1, tiled=True)]
  transfers between devices with their start and end apart: 4 -> 10, of which waited for: 4 -> 8; matrix products, arithmetic and copies ran while one was open for 2% -> 5% of each run, Pallas kernels for 0% -> 0%
where the time goes in v1:
time: 259 us
  waiting for transfers between devices  166 us (64%)
  blocking collectives  62.9 us (24%)
  between operations  14.7 us (6%)
  local copies, waits for them, and re-layouts  5.29 us (2%)
  matrix products  5.04 us (2%)
  other arithmetic  3.93 us (2%)
    reduce_scatter x2, waiting for transfers between devices, sum_rows(): return lax.psum_scatter(direct, 'col', scatter_dimension=1, tiled=True)  130 us
    all_gather x2, blocking collectives, gather_rowset(): return lax.all_gather(vec, 'col', axis=1, tiled=True)  62.9 us
    reduce_scatter x2, waiting for transfers between devices, sum_cols(): return lax.psum_scatter(mirror, 'row', scatter_dimension=1, tiled=True)  25.3 us
    ppermute x6, waiting for transfers between devices, press_the_panels(): oldest[nth] = lax.ppermute(oldest[nth + 1], 'row', lanes)  10.7 us
  transfers between devices with their start and end apart: 10, of which 8 were waited for; matrix products, arithmetic and copies ran while one was open for 5% of the time, Pallas kernels for 0%

profile of v1, /device:TPU:0, one launch (start us, length us, event | category | flops | bytes accessed | tf_op | source)
XLA Modules:
  0.0 259.0 jit_solution(14689056998107084794)
XLA Ops:
  7.2 0.0 copy-start
  7.2 0.0 copy-start.3
  7.2 0.0 reduce-scatter.7.cloned.1.call-start
  7.2 0.5 collective-permute-start
  7.7 32.2 %all_gather.6 = bf16[32,2048]{1,0:T(8,128)(2,1)S(1)} all-gather(bf16[32,256]{1,0:T(8,128)(2,1)} %param.11), channel_id=1, replica_groups=mesh['row'=4,'col'=8] {'col'}, dimensions={1}, use_global_device_ids=true | all-gather | bytes 147456 | tf_op jit(solution)/shard_map/all_gather | solution.py:51
  40.0 0.7 compare_select_fusion
  40.6 0.7 compare_and_fusion
  42.0 0.6 gather_fusion.1
  42.6 0.0 copy-start.2
  42.6 0.0 copy-done
  42.6 0.5 convolution_bitcast_fusion.2
  43.1 0.0 copy-done.3
  43.1 0.7 fusion.4
  43.7 0.0 copy-start.4
  43.8 0.7 copy.20
  44.5 0.0 reduce-scatter.7.cloned.1.call-update
  44.5 0.0 reduce-scatter.5.cloned.1.call-start
  44.5 0.0 collective-permute-done
  44.5 0.1 collective-permute-start.1
  44.6 3.1 %collective-permute-done.1 = bf16[32,256]{1,0:T(8,128)(2,1)S(1)} collective-permute-done((bf16[32,256]{1,0:T(8,128)(2,1)S(1)}, bf16[32,256]{1,0:T(8,128)(2,1)S(1)}, u32[]{:S(2)}, u32[]{:S(2)}) %collective-permute-start.1) | collective-permute-done | bytes 16416 | tf_op jit(solution)/shard_map/ppermute | solution.py:13
  47.7 0.0 collective-permute-start.2
  47.8 3.1 %collective-permute-done.2 = bf16[32,256]{1,0:T(8,128)(2,1)S(1)} collective-permute-done((bf16[32,256]{1,0:T(8,128)(2,1)S(1)}, bf16[32,256]{1,0:T(8,128)(2,1)S(1)}, u32[]{:S(2)}, u32[]{:S(2)}) %collective-permute-start.2) | collective-permute-done | bytes 16416 | tf_op jit(solution)/shard_map/ppermute | solution.py:13
  50.9 0.0 copy-done.2
  50.9 0.2 fusion.34
  51.1 0.6 gather_fusion
  51.7 0.7 convolution_bitcast_fusion.3
  52.4 0.0 copy-done.4
  52.5 0.7 fusion.6
  53.1 0.8 copy.19
  53.9 0.0 reduce-scatter.5.cloned.1.call-update
  53.9 0.0 reduce-scatter.11.cloned.1.call-start
  54.0 11.1 %reduce-scatter.7.cloned.1.call-done = f32[32,256]{1,0:T(8,128)} async-done(((f32[32,1024]{1,0:T(8,128)}), f32[32,256]{1,0:T(8,128)}) %reduce-scatter.7.cloned.1.call-update) | async-done | bytes 32784 | tf_op jit(solution)/shard_map/reduce_scatter | solution.py:47
  65.1 65.4 %reduce-scatter.5.cloned.1.call-done = f32[32,256]{1,0:T(8,128)} async-done(((f32[32,2048]{1,0:T(8,128)}), f32[32,256]{1,0:T(8,128)}) %reduce-scatter.5.cloned.1.call-update) | async-done | bytes 32784 | tf_op jit(solution)/shard_map/reduce_scatter | solution.py:43
  130.5 0.8 add_convert_fusion
  131.3 0.0 copy-start.1
  131.3 0.1 collective-permute-start.3
  131.3 30.7 %all_gather.7 = bf16[32,2048]{1,0:T(8,128)(2,1)S(1)} all-gather(bf16[32,256]{1,0:T(8,128)(2,1)S(1)} %add_convert_fusion), channel_id=1, replica_groups=mesh['row'=4,'col'=8] {'col'}, dimensions={1}, use_global_device_ids=true | all-gather | bytes 147456 | tf_op jit(solution)/shard_map/all_gather | solution.py:51
  162.0 0.6 gather_fusion.3
  162.6 0.0 collective-permute-done.3
  162.6 0.1 collective-permute-start.4
  162.7 0.5 convolution_bitcast_fusion
  163.2 2.7 %collective-permute-done.4 = bf16[32,256]{1,0:T(8,128)(2,1)S(1)} collective-permute-done((bf16[32,256]{1,0:T(8,128)(2,1)S(1)}, bf16[32,256]{1,0:T(8,128)(2,1)S(1)}, u32[]{:S(2)}, u32[]{:S(2)}) %collective-permute-start.4) | collective-permute-done | bytes 16416 | tf_op jit(solution)/shard_map/ppermute | solution.py:13
  165.8 0.0 collective-permute-start.5
  165.8 0.7 fusion
  166.5 0.7 copy.22
  167.2 0.0 reduce-scatter.11.cloned.1.call-update
  167.2 0.0 reduce-scatter.9.cloned.1.call-start
  167.3 1.7 collective-permute-done.5
  169.0 0.0 copy-done.1
  169.0 0.2 fusion.27
  169.2 0.6 gather_fusion.2
  169.8 0.7 convolution_bitcast_fusion.1
  170.5 0.7 fusion.2
  171.2 0.8 copy.21
  172.0 0.0 reduce-scatter.9.cloned.1.call-update
  172.0 14.1 %reduce-scatter.11.cloned.1.call-done = f32[32,256]{1,0:T(8,128)} async-done(((f32[32,1024]{1,0:T(8,128)}), f32[32,256]{1,0:T(8,128)}) %reduce-scatter.11.cloned.1.call-update) | async-done | bytes 32784 | tf_op jit(solution)/shard_map/reduce_scatter | solution.py:47
  186.1 64.9 %reduce-scatter.9.cloned.1.call-done = f32[32,256]{1,0:T(8,128)} async-done(((f32[32,2048]{1,0:T(8,128)}), f32[32,256]{1,0:T(8,128)}) %reduce-scatter.9.cloned.1.call-update) | async-done | bytes 32784 | tf_op jit(solution)/shard_map/reduce_scatter | solution.py:43
  251.1 1.4 subtract_convert_fusion
  (8 shorter events, 0.1 us)
Async XLA Ops:
  7.2 35.4 %copy-start = (bf16[16,256,256]{2,1,0:T(8,128)(2,1)S(1)}, bf16[16,256,256]{2,1,0:T(8,128)(2,1)}, u32[]{:S(2)}) copy-start(bf16[16,256,256]{2,1,0:T(8,128)(2,1)} %param.12) | copy-start | bytes 6291460
  7.2 35.9 %copy-start.3 = (s32[16]{0:T(128)S(1)}, s32[16]{0:T(128)}, u32[]{:S(2)}) copy-start(s32[16]{0:T(128)} %param.14) | copy-start | bytes 196
  7.2 57.9 %reduce-scatter.7.cloned.1.call-start = ((), (), s32[]{:S(2)}) async-start(), calls=%async_computation.5 | async-start | bytes 163840 | tf_op jit(solution)/shard_map/reduce_scatter | solution.py:47
  7.2 37.3 %collective-permute-start = (bf16[32,256]{1,0:T(8,128)(2,1)}, bf16[32,256]{1,0:T(8,128)(2,1)S(1)}, u32[]{:S(2)}, u32[]{:S(2)}) collective-permute-start(bf16[32,256]{1,0:T(8,128)(2,1)} %param.11), channel_id=1, source_target_pairs={{0,8},{8,16},{16,24},{24,0},{1,9},{9,17},{17,25},{25,1},{2,10},{10... | collective-permute-start | bytes 49160 | tf_op jit(solution)/shard_map/ppermute | solution.py:13
  42.6 8.4 %copy-start.2 = (bf16[32,256]{1,0:T(8,128)(2,1)S(1)}, bf16[32,256]{1,0:T(8,128)(2,1)}, u32[]{:S(2)}) copy-start(bf16[32,256]{1,0:T(8,128)(2,1)} %param.11) | copy-start | bytes 49156
  43.7 8.7 %copy-start.4 = (s32[16]{0:T(128)S(1)}, s32[16]{0:T(128)}, u32[]{:S(2)}) copy-start(s32[16]{0:T(128)} %param.13) | copy-start | bytes 196
  44.5 86.0 %reduce-scatter.5.cloned.1.call-start = ((), (), s32[]{:S(2)}) async-start(), calls=%async_computation.4 | async-start | bytes 294912 | tf_op jit(solution)/shard_map/reduce_scatter | solution.py:43
  44.5 3.2 %collective-permute-start.1 = (bf16[32,256]{1,0:T(8,128)(2,1)S(1)}, bf16[32,256]{1,0:T(8,128)(2,1)S(1)}, u32[]{:S(2)}, u32[]{:S(2)}) collective-permute-start(bf16[32,256]{1,0:T(8,128)(2,1)S(1)} %collective-permute-done), channel_id=1, source_target_pairs={{0,8},{8,16},{16,24},{24,0},{1,9},{9,17},{17,25},{25,1},{2,10},{10... | collective-permute-start | bytes 49160 | tf_op jit(solution)/shard_map/ppermute | solution.py:13
  47.7 3.2 %collective-permute-start.2 = (bf16[32,256]{1,0:T(8,128)(2,1)S(1)}, bf16[32,256]{1,0:T(8,128)(2,1)S(1)}, u32[]{:S(2)}, u32[]{:S(2)}) collective-permute-start(bf16[32,256]{1,0:T(8,128)(2,1)S(1)} %collective-permute-done.1), channel_id=1, source_target_pairs={{0,8},{8,16},{16,24},{24,0},{1,9},{9,17},{17,25},{25,1},{2,10},{10... | collective-permute-start | bytes 49160 | tf_op jit(solution)/shard_map/ppermute | solution.py:13
  53.9 132.2 %reduce-scatter.11.cloned.1.call-start = ((), (), s32[]{:S(2)}) async-start(), calls=%async_computation.7 | async-start | bytes 163840 | tf_op jit(solution)/shard_map/reduce_scatter | solution.py:47
  131.3 37.7 %copy-start.1 = (bf16[32,256]{1,0:T(8,128)(2,1)}, bf16[32,256]{1,0:T(8,128)(2,1)S(1)}, u32[]{:S(2)}) copy-start(bf16[32,256]{1,0:T(8,128)(2,1)S(1)} %add_convert_fusion) | copy-start | bytes 49156
  131.3 31.3 %collective-permute-start.3 = (bf16[32,256]{1,0:T(8,128)(2,1)S(1)}, bf16[32,256]{1,0:T(8,128)(2,1)S(1)}, u32[]{:S(2)}, u32[]{:S(2)}) collective-permute-start(bf16[32,256]{1,0:T(8,128)(2,1)S(1)} %add_convert_fusion), channel_id=1, source_target_pairs={{0,8},{8,16},{16,24},{24,0},{1,9},{9,17},{17,25},{25,1},{2,10},{10... | collective-permute-start | bytes 49160 | tf_op jit(solution)/shard_map/ppermute | solution.py:13
  162.6 3.2 %collective-permute-start.4 = (bf16[32,256]{1,0:T(8,128)(2,1)S(1)}, bf16[32,256]{1,0:T(8,128)(2,1)S(1)}, u32[]{:S(2)}, u32[]{:S(2)}) collective-permute-start(bf16[32,256]{1,0:T(8,128)(2,1)S(1)} %collective-permute-done.3), channel_id=1, source_target_pairs={{0,8},{8,16},{16,24},{24,0},{1,9},{9,17},{17,25},{25,1},{2,10},{10... | collective-permute-start | bytes 49160 | tf_op jit(solution)/shard_map/ppermute | solution.py:13
  165.8 3.2 %collective-permute-start.5 = (bf16[32,256]{1,0:T(8,128)(2,1)S(1)}, bf16[32,256]{1,0:T(8,128)(2,1)S(1)}, u32[]{:S(2)}, u32[]{:S(2)}) collective-permute-start(bf16[32,256]{1,0:T(8,128)(2,1)S(1)} %collective-permute-done.4), channel_id=1, source_target_pairs={{0,8},{8,16},{16,24},{24,0},{1,9},{9,17},{17,25},{25,1},{2,10},{10... | collective-permute-start | bytes 49160 | tf_op jit(solution)/shard_map/ppermute | solution.py:13
  167.2 83.9 %reduce-scatter.9.cloned.1.call-start = ((), (), s32[]{:S(2)}) async-start(), calls=%async_computation.6 | async-start | bytes 294912 | tf_op jit(solution)/shard_map/reduce_scatter | solution.py:43
Sparse Core Ops, SparseCore 0:
  44.6 20.4 reduce-scatter.6
  68.8 61.6 reduce-scatter.4
  167.3 18.7 reduce-scatter.10
  189.3 61.6 reduce-scatter.8
